TPU v7x, 32 devices: a whole 2x2x4 slice. The times are simulated.
32 devices in a mesh: aux: 4 (over x, core), cd: 4 (over z), ab: 2 (over y).
Axes of the slice: x: 2, y: 2, z: 4, core: 2. Of those that a mesh axis runs over, the one named last changes fastest.
Arguments:
- left_integrals: bfloat16 [4, 2048, 2048], P('cd', 'ab', 'aux'), may hold values from -6 to 6
- right_integrals: bfloat16 [2, 2048, 2048], P('ab', 'cd', 'aux'), may hold values from -6 to 6
- metric_factor: bfloat16 [2048, 2048], P('aux'), may hold values from -0.125 to 0.125
- amplitudes: bfloat16 [32, 2048, 2048], P(None, 'ab', 'cd'), may hold values from -6.4373016e-05 to 6.4373016e-05
- tile_sizes: int32 [16], replicated, may hold values from 1 to 256, 2048 in all
- pair_mask: int32 [16, 16], replicated, may hold values 0 or 1
Outputs:
- ladder_residual: float32 [4, 2, 32], P('cd', 'ab')
Inputs may be any that keep to these rules, and one draw needn't show every extreme that they name: `tile_sizes`: the 16 tile sizes sum to 2048.
All inputs are finite; a program needn't handle non-finite values.
Results may differ from a plain program's by a relative error of at most 0.0038.
Values may be sent and summed in bfloat16 or wider, within the bound.
A program may use at most 128 MiB of HBM per device.

v0:
```python
import jax
import jax.numpy as jnp
from jax import lax
from jax.sharding import PartitionSpec as P


def region_keep(tile_sizes, pair_mask, c_offset, c_count, d_offset, d_count):
    tile_end = jnp.cumsum(tile_sizes)
    tile_range = jnp.arange(tile_end.shape[0], dtype=jnp.int32)

    def onehot(offset, count):
        positions = offset + jnp.arange(count, dtype=jnp.int32)
        tile_index = jnp.sum((positions[:, None] >= tile_end[None, :]).astype(jnp.int32), axis=1)
        return (tile_index[:, None] == tile_range[None, :]).astype(jnp.float32)

    left_hot = onehot(c_offset, c_count)
    right_hot = onehot(d_offset, d_count)
    mask_table = pair_mask.astype(jnp.float32)
    inner = jnp.dot(left_hot, mask_table, precision=lax.Precision.HIGHEST)
    return jnp.dot(inner, right_hot.T, precision=lax.Precision.HIGHEST)


def ladder_terms(left_piece, right_all, kept):
    aux_count = left_piece.shape[0]
    b_count = right_all.shape[1]
    d_width = right_all.shape[2]
    right_flat = right_all.reshape(aux_count, b_count * d_width)

    def one_virtual(left_slab):
        ladder = lax.dot_general(
            left_slab, right_flat, (((0,), (0,)), ((), ())), preferred_element_type=jnp.float32
        )
        ladder = ladder.astype(jnp.bfloat16).reshape(-1, b_count, d_width)
        total = lax.dot_general(
            ladder, kept, (((0, 2), (1, 2)), ((), ())), preferred_element_type=jnp.float32
        )
        return total

    return lax.map(one_virtual, jnp.moveaxis(left_piece, 1, 0))


def body(left_integrals, right_integrals, metric_factor, amplitudes, tile_sizes, pair_mask):
    aux_local = metric_factor.shape[0]
    aux_total = metric_factor.shape[1]
    a_local = left_integrals.shape[0]
    b_local = right_integrals.shape[0]
    c_width = amplitudes.shape[1]
    d_width = amplitudes.shape[2]
    pair_count = amplitudes.shape[0]
    c_offset = lax.axis_index("ab") * c_width
    d_offset = lax.axis_index("cd") * d_width
    left_count = a_local * c_width
    stacked = jnp.concatenate(
        [left_integrals.reshape(-1, aux_local), right_integrals.reshape(-1, aux_local)], axis=0
    )
    share = aux_total // lax.axis_size("aux")
    fitted = lax.psum_scatter(
        lax.dot_general(
            metric_factor, stacked, (((0,), (1,)), ((), ())), preferred_element_type=jnp.float32
        ),
        "aux",
        scatter_dimension=0,
        tiled=True,
    ).astype(jnp.bfloat16)
    left_fit = fitted[:, :left_count].reshape(share, a_local, c_width)
    right_fit = fitted[:, left_count:].reshape(share, b_local, d_width)
    right_all = lax.all_gather(right_fit, "ab", axis=1, tiled=True)
    keep_mask = region_keep(tile_sizes, pair_mask, c_offset, c_width, d_offset, d_width)
    kept = amplitudes * keep_mask.astype(jnp.bfloat16)[None]
    partial_sums = ladder_terms(lax.all_gather(left_fit, "cd", axis=1, tiled=True), right_all, kept)
    flat_terms = partial_sums.reshape(-1, pair_count)
    owned = lax.psum_scatter(flat_terms, ("cd", "ab"), scatter_dimension=0, tiled=True)
    totals = lax.psum(owned, "aux")
    return totals.reshape(a_local, b_local, pair_count)


def solution(mesh):
    return jax.shard_map(
        body,
        mesh=mesh,
        in_specs=(
            P("cd", "ab", "aux"),
            P("ab", "cd", "aux"),
            P("aux", None),
            P(None, "ab", "cd"),
            P(),
            P(),
        ),
        out_specs=P("cd", "ab", None),
        check_vma=False,
    )
```

profile of v0, /device:TPU:0, one launch (start us, length us, event | category | flops | bytes accessed | tf_op | source)
XLA Modules:
  0.0 353.8 jit_solution(16906253457313340899)
XLA Ops:
  6.5 1.6 copy-done
  8.1 7.8 %convolution_bitcast_fusion.1 = f32[2048,1536]{0,1:T(8,128)} fusion(bf16[512,2048]{1,0:T(8,128)(2,1)S(1)} %copy-done, bf16[512,512]{1,0:T(8,128)(2,1)} %bitcast.43, bf16[1024,512]{1,0:T(8,128)(2,1)} %bitcast.42), kind=kOutput, calls=%fused_computation.7 | convolution fusion | flops 3224371200 | bytes 16252928 | tf_op jit(solution)/shard_map/dot_general | solution.py:58
  16.0 100.0 %reduce-scatter.2.cloned.1.call-done = f32[512,1536]{0,1:T(8,128)} async-done(((f32[2048,1536]{0,1:T(8,128)}), f32[512,1536]{0,1:T(8,128)}) %reduce-scatter.2.cloned.1.call-update) | async-done | bytes 3145744 | tf_op jit(solution)/shard_map/reduce_scatter | solution.py:57
  116.0 2.1 convert_element_type.20
  121.6 1.1 convolution_convert_fusion.1
  122.7 29.4 %copy_multiply_fusion = bf16[32,1024,512]{2,0,1:T(8,128)(2,1)} fusion(bf16[32,1024,512]{2,1,0:T(8,128)(2,1)} %param.11, bf16[1024,512]{1,0:T(8,128)(2,1)S(1)} %convolution_convert_fusion.1), kind=kLoop, calls=%fused_computation.6 | loop fusion | flops 16777216 | bytes 68157440 | tf_op jit(solution)/shard_map/mul | solution.py:69
  152.1 1.5 copy.26
  153.6 69.1 %all-gather.5.cloned.1.call-done = bf16[512,4096]{0,1:T(8,128)(2,1)} async-done(((bf16[512,1024]{0,1:T(8,128)(2,1)}), bf16[512,4096]{0,1:T(8,128)(2,1)}) %all-gather.5.cloned.1.call-update) | async-done | bytes 4194320 | tf_op jit(solution)/shard_map/all_gather | solution.py:70
  222.8 6.3 %copy.23 = bf16[512,4,1024]{2,0,1:T(8,128)(2,1)} copy(bf16[512,4,1024]{0,2,1:T(8,128)(2,1)} %bitcast.38) | data formatting | bytes 8388608 | tf_op jit(solution)/shard_map/all_gather | solution.py:70
  229.1 92.4 %while.10 = (s32[]{:T(128)}, f32[4,2,32]{2,1,0:T(2,128)S(1)}, bf16[4,512,1024]{2,1,0:T(8,128)(2,1)}, bf16[512,1024]{1,0:T(8,128)(2,1)S(1)}, bf16[32,1024,512]{2,0,1:T(8,128)(2,1)}, /*index=5*/s32[]{:T(128)}) while((s32[]{:T(128)}, f32[4,2,32]{2,1,0:T(2,128)S(1)}, bf16[4,512,1024]{2,1,0:T(8,128)(2,1)}, bf16[512,1024]{1,0:T(8,128)(2,1)S(1)}, ...), condition=%wide.region_5.6_spmd, body=%wide.region_4.5_spmd.sunk | while | flops 1141899264 | bytes 44041300 | solution.py:39
  229.1 3.8 %convolution_convert_fusion.3 = bf16[1024,1024]{0,1:T(8,128)(2,1)} fusion(bf16[512,1024]{1,0:T(8,128)(2,1)S(1)} %get-tuple-element.109, bf16[4,512,1024]{2,1,0:T(8,128)(2,1)} %get-tuple-element.108, s32[]{:T(128)S(6)} %copy.33), kind=kOutput, calls=%fused_computation.clone.1 | convolution fusion | flops 1074790400 | bytes 4194308 | tf_op jit(solution)/shard_map/while/body/eval_jaxpr/dot_general | solution.py:30
  232.9 4.8 %copy.29 = bf16[1024,2,512]{2,1,0:T(2,128)(2,1)S(1)} copy(bf16[1024,2,512]{0,2,1:T(8,128)(2,1)} %bitcast.37) | data formatting | bytes 4194304 | tf_op jit(solution)/shard_map/while/body/eval_jaxpr/reshape | solution.py:33
  237.8 14.4 %fusion.26 = f32[4,2,32]{2,1,0:T(2,128)S(1)} fusion(f32[4,2,32]{2,1,0:T(2,128)S(1)} %get-tuple-element.101, s32[]{:T(128)S(6)} %copy.33, bf16[1024,2,512]{2,1,0:T(2,128)(2,1)S(1)} %copy.29, bf16[32,1024,512]{2,0,1:T(8,128)(2,1)} %get-tuple-element.110), kind=kOutput, calls=%fused_computation.2.clone.1 | convolution fusion | flops 67108864 | bytes 35652612 | tf_op jit(solution)/shard_map/while/body/eval_jaxpr/dot_general | solution.py:34
  252.2 3.9 %convolution_convert_fusion.3 = bf16[1024,1024]{0,1:T(8,128)(2,1)} fusion(bf16[512,1024]{1,0:T(8,128)(2,1)S(1)} %get-tuple-element.109, bf16[4,512,1024]{2,1,0:T(8,128)(2,1)} %get-tuple-element.108, s32[]{:T(128)S(6)} %copy.33), kind=kOutput, calls=%fused_computation.clone.1 | convolution fusion | flops 1074790400 | bytes 4194308 | tf_op jit(solution)/shard_map/while/body/eval_jaxpr/dot_general | solution.py:30
  256.1 4.8 %copy.29 = bf16[1024,2,512]{2,1,0:T(2,128)(2,1)S(1)} copy(bf16[1024,2,512]{0,2,1:T(8,128)(2,1)} %bitcast.37) | data formatting | bytes 4194304 | tf_op jit(solution)/shard_map/while/body/eval_jaxpr/reshape | solution.py:33
  260.9 14.4 %fusion.26 = f32[4,2,32]{2,1,0:T(2,128)S(1)} fusion(f32[4,2,32]{2,1,0:T(2,128)S(1)} %get-tuple-element.101, s32[]{:T(128)S(6)} %copy.33, bf16[1024,2,512]{2,1,0:T(2,128)(2,1)S(1)} %copy.29, bf16[32,1024,512]{2,0,1:T(8,128)(2,1)} %get-tuple-element.110), kind=kOutput, calls=%fused_computation.2.clone.1 | convolution fusion | flops 67108864 | bytes 35652612 | tf_op jit(solution)/shard_map/while/body/eval_jaxpr/dot_general | solution.py:34
  275.3 3.9 %convolution_convert_fusion.3 = bf16[1024,1024]{0,1:T(8,128)(2,1)} fusion(bf16[512,1024]{1,0:T(8,128)(2,1)S(1)} %get-tuple-element.109, bf16[4,512,1024]{2,1,0:T(8,128)(2,1)} %get-tuple-element.108, s32[]{:T(128)S(6)} %copy.33), kind=kOutput, calls=%fused_computation.clone.1 | convolution fusion | flops 1074790400 | bytes 4194308 | tf_op jit(solution)/shard_map/while/body/eval_jaxpr/dot_general | solution.py:30
  279.2 4.8 %copy.29 = bf16[1024,2,512]{2,1,0:T(2,128)(2,1)S(1)} copy(bf16[1024,2,512]{0,2,1:T(8,128)(2,1)} %bitcast.37) | data formatting | bytes 4194304 | tf_op jit(solution)/shard_map/while/body/eval_jaxpr/reshape | solution.py:33
  284.0 14.4 %fusion.26 = f32[4,2,32]{2,1,0:T(2,128)S(1)} fusion(f32[4,2,32]{2,1,0:T(2,128)S(1)} %get-tuple-element.101, s32[]{:T(128)S(6)} %copy.33, bf16[1024,2,512]{2,1,0:T(2,128)(2,1)S(1)} %copy.29, bf16[32,1024,512]{2,0,1:T(8,128)(2,1)} %get-tuple-element.110), kind=kOutput, calls=%fused_computation.2.clone.1 | convolution fusion | flops 67108864 | bytes 35652612 | tf_op jit(solution)/shard_map/while/body/eval_jaxpr/dot_general | solution.py:34
  298.4 3.9 %convolution_convert_fusion.3 = bf16[1024,1024]{0,1:T(8,128)(2,1)} fusion(bf16[512,1024]{1,0:T(8,128)(2,1)S(1)} %get-tuple-element.109, bf16[4,512,1024]{2,1,0:T(8,128)(2,1)} %get-tuple-element.108, s32[]{:T(128)S(6)} %copy.33), kind=kOutput, calls=%fused_computation.clone.1 | convolution fusion | flops 1074790400 | bytes 4194308 | tf_op jit(solution)/shard_map/while/body/eval_jaxpr/dot_general | solution.py:30
  302.3 4.8 %copy.29 = bf16[1024,2,512]{2,1,0:T(2,128)(2,1)S(1)} copy(bf16[1024,2,512]{0,2,1:T(8,128)(2,1)} %bitcast.37) | data formatting | bytes 4194304 | tf_op jit(solution)/shard_map/while/body/eval_jaxpr/reshape | solution.py:33
  307.1 14.4 %fusion.26 = f32[4,2,32]{2,1,0:T(2,128)S(1)} fusion(f32[4,2,32]{2,1,0:T(2,128)S(1)} %get-tuple-element.101, s32[]{:T(128)S(6)} %copy.33, bf16[1024,2,512]{2,1,0:T(2,128)(2,1)S(1)} %copy.29, bf16[32,1024,512]{2,0,1:T(8,128)(2,1)} %get-tuple-element.110), kind=kOutput, calls=%fused_computation.2.clone.1 | convolution fusion | flops 67108864 | bytes 35652612 | tf_op jit(solution)/shard_map/while/body/eval_jaxpr/dot_general | solution.py:34
  321.6 19.0 %all-reduce = f32[8,32]{1,0:T(8,128)S(1)} all-reduce(f32[8,32]{1,0:T(8,128)S(1)} %bitcast.40), channel_id=5, replica_groups=mesh['aux'=4,'cd'=4,'ab'=2] {'cd','ab'}, use_global_device_ids=true, to_apply=%region_6.7.clone | all-reduce | flops 256 | bytes 2048
  341.1 6.2 %psum.7 = f32[1,1,32]{2,1,0:T(1,128)} all-reduce(f32[1,1,32]{2,1,0:T(1,128)S(1)} %dynamic-slice_bitcast_fusion), channel_id=1, replica_groups=mesh['aux'=4,'cd'=4,'ab'=2] {'aux'}, use_global_device_ids=true, to_apply=%region_7.8 | all-reduce | flops 32 | bytes 256 | tf_op jit(solution)/shard_map/psum | solution.py:73
  (29 shorter events, 4.0 us)
Async XLA Ops:
  6.5 1.6 copy-start
  6.5 109.4 %reduce-scatter.2.cloned.1.call-start = ((), (), s32[]{:S(2)}) async-start(), calls=%async_computation.1 | async-start | bytes 15728640 | tf_op jit(solution)/shard_map/reduce_scatter | solution.py:57
  15.9 136.2 %all-gather.7.cloned.1.call-start = ((), (), s32[]{:S(2)}) async-start(), calls=%async_computation.3 | async-start | bytes 1572864 | tf_op jit(solution)/shard_map/all_gather | solution.py:67
  118.1 2.0 copy-start.2
  118.1 2.3 copy-start.4
  118.1 3.0 copy-start.3
  119.0 103.8 %all-gather.5.cloned.1.call-start = ((), (), s32[]{:S(2)}) async-start(), calls=%async_computation.2 | async-start | bytes 5242880 | tf_op jit(solution)/shard_map/all_gather | solution.py:70
  321.6 25.7 %copy-start.1 = (bf16[512,2048]{1,0:T(8,128)(2,1)S(1)}, bf16[512,2048]{1,0:T(8,128)(2,1)}, u32[]{:S(2)}) copy-start(bf16[512,2048]{1,0:T(8,128)(2,1)} %param.10) | copy-start | bytes 6291460
Sparse Core Ops, SparseCore 0:
  16.1 99.8 reduce-scatter.1
  119.1 21.2 all-gather.6
  142.0 80.7 all-gather.4
where the time goes:
time: 355 us; the launch traced here: 354 us
  waiting for transfers between devices  169 us (48%)
  matrix products  82.5 us (23%)
  local copies, waits for them, and re-layouts  31.8 us (9%)
  other arithmetic  31.8 us (9%)
  blocking collectives  25.1 us (7%)
  between operations  13.2 us (4%)
    reduce_scatter x1, waiting for transfers between devices, body(): lax.psum_scatter(lax.dot_general(metric_factor, stacked, (((0,), (1,)), (...  100 us
    all_gather x1, waiting for transfers between devices, body(): lax.all_gather(left_fit, 'cd', axis=1, tiled=True)  69.1 us
    dot_general x4, matrix products, one_virtual(): lax.dot_general(ladder, kept, (((0, 2), (1, 2)), ((), ())), preferred_ele...  57.7 us
    mul x1, other arithmetic, body(): kept = amplitudes * keep_mask.astype(jnp.bfloat16)[None]  29.4 us
    reshape x4, local copies, waits for them, and re-layouts, one_virtual(): ladder = ladder.astype(jnp.bfloat16).reshape(-1, b_count, d_width)  19.3 us
    unnamed x1, blocking collectives  19 us
    dot_general x4, matrix products, one_virtual(): lax.dot_general(left_slab, right_flat, (((0,), (0,)), ((), ())), preferre...  15.4 us
    dot_general x1, matrix products, body(): lax.dot_general(metric_factor, stacked, (((0,), (1,)), ((), ())), preferr...  7.79 us
  transfers between devices with their start and end apart: 3, of which 2 were waited for; matrix products, arithmetic and copies ran while one was open for 10% of the time, Pallas kernels for 0%

commit v1 on v0

v1 whole, which is shorter than its diff:
```python
import functools

import jax
import jax.numpy as jnp
from jax import lax
from jax.experimental import pallas as pl
from jax.experimental.pallas import tpu as pltpu
from jax.sharding import PartitionSpec as P

NT = (((1,), (1,)), ((), ()))
NN = (((1,), (0,)), ((), ()))
GROUP = 16
MESH = pl.DeviceIdType.MESH


def dot(x, y, dims):
    return lax.dot_general(x, y, dims, preferred_element_type=jnp.float32)


def kernel(A, Z, B, CB, sizes, left, right, metric, pair, amp, out,
           gathered, send1, got1, own, chip, got2, t_hi, t_lo, fit, amps, ladder, acc,
           hot_rows, hot_cols, part, got_z, mine, got_ab,
           z_send, z_recv, s_send, s_recv, x_send, x_recv, t_send, t_recv,
           u_send, u_recv, amp_sem, own_sem, fz_send, fz_recv, fa_send, fa_recv):
    aux, z, y = lax.axis_index("aux"), lax.axis_index("cd"), lax.axis_index("ab")
    C, PW = left.shape
    D = right.shape[0]
    Q = metric.shape[1]
    I = amp.shape[0]
    T = pair.shape[0]
    NC = C // CB
    H = D // 2
    QB = min(512, Q)
    core = lax.rem(aux, 2)
    sibling = aux + 1 - 2 * core

    def rcopy(src, dst, ss, rs, dev):
        return pltpu.make_async_remote_copy(src_ref=src, dst_ref=dst, send_sem=ss, recv_sem=rs,
                                            device_id=dev, device_id_type=MESH)

    def plane_peer(o):
        flat = lax.rem(aux * B + y + o, A * B)
        return {"aux": flat // B, "ab": lax.rem(flat, B)}

    def amp_copy(k, slot):
        rows = pl.ds(pl.multiple_of(k * CB, CB), CB)
        return pltpu.make_async_copy(amp.at[:, rows, :], amps.at[slot], amp_sem.at[slot])

    barrier = pltpu.get_barrier_semaphore()
    for o in range(1, Z):
        pl.semaphore_signal(barrier, inc=1, device_id={"cd": lax.rem(z + o, Z)}, device_id_type=MESH)
    for o in range(1, A * B):
        pl.semaphore_signal(barrier, inc=1, device_id=plane_peer(o), device_id_type=MESH)
    pl.semaphore_wait(barrier, Z - 1 + A * B - 1)

    def chunk(k):
        return pl.ds(pl.multiple_of(k * CB, CB), CB)

    def push(src, o, k, way):
        dev = {"cd": z + 1} if way == 0 else {"cd": z - 1}
        return rcopy(src, gathered.at[o, chunk(k)], z_send.at[way, o, k], z_recv.at[o, k], dev)

    def first(k, c):
        @pl.when(z < Z - 1)
        def _():
            push(left.at[chunk(k)], z, k, 0).start()

        @pl.when(z > 0)
        def _():
            push(left.at[chunk(k)], z, k, 1).start()
        return c

    lax.fori_loop(0, NC, first, 0)
    own_copy = pltpu.make_async_copy(left, gathered.at[z], own_sem)
    own_copy.start()
    amp_copy(0, 0).start()
    if NC > 1:
        amp_copy(1, 1).start()

    def relay_chunk(h, k):
        @pl.when(z - h >= 0)
        def _():
            o = z - h
            push(gathered.at[o, chunk(k)], o, k, 0).wait_recv()
            if h < Z - 1:
                @pl.when(z < Z - 1)
                def _():
                    push(gathered.at[o, chunk(k)], o, k, 0).start()

        @pl.when(z + h < Z)
        def _():
            o = z + h
            push(gathered.at[o, chunk(k)], o, k, 1).wait_recv()
            if h < Z - 1:
                @pl.when(z > 0)
                def _():
                    push(gathered.at[o, chunk(k)], o, k, 1).start()

    def relay(h):
        def step(k, c):
            relay_chunk(h, k)
            return c
        lax.fori_loop(0, NC, step, 0)

    mine_rows = pl.ds(pl.multiple_of(core * H, H), H)
    other_rows = pl.ds(pl.multiple_of((1 - core) * H, H), H)

    def cols(j):
        return pl.ds(pl.multiple_of(j * QB, QB), QB)

    def fit_other(j, c):
        send1[:, cols(j)] = dot(right[other_rows, :], metric[:, cols(j)], NN).astype(jnp.bfloat16)
        return c

    lax.fori_loop(0, Q // QB, fit_other, 0)
    pair_copy = rcopy(send1, got1, s_send, s_recv, {"aux": sibling})
    pair_copy.start()

    def fit_own(j, c):
        own[:, cols(j)] = dot(right[mine_rows, :], metric[:, cols(j)], NN)
        return c

    lax.fori_loop(0, Q // QB, fit_own, 0)
    pair_copy.wait()

    def add_pair(j, c):
        total = own[:, cols(j)] + got1[:, cols(j)].astype(jnp.float32)
        own[:, cols(j)] = total
        chip[:, cols(j)] = total.astype(jnp.bfloat16)
        return c

    lax.fori_loop(0, Q // QB, add_pair, 0)
    x_copies = [rcopy(chip, got2.at[n], x_send.at[n], x_recv.at[n], {"aux": lax.rem(aux + 2 * n + 2, A)})
                for n in range(A // 2 - 1)]
    for cp in x_copies:
        cp.start()

    rows_at = y * C + lax.broadcasted_iota(jnp.int32, (C, T), 0)
    rows_tile = lax.broadcasted_iota(jnp.int32, (C, T), 1)
    cols_at = z * D + lax.broadcasted_iota(jnp.int32, (T, D), 1)
    cols_tile = lax.broadcasted_iota(jnp.int32, (T, D), 0)
    row_hot = jnp.zeros((C, T), jnp.float32)
    col_hot = jnp.zeros((T, D), jnp.float32)
    low = jnp.int32(0)
    for t in range(T):
        high = low + sizes[t]
        row_hot = jnp.where((rows_tile == t) & (rows_at >= low) & (rows_at < high), 1.0, row_hot)
        col_hot = jnp.where((cols_tile == t) & (cols_at >= low) & (cols_at < high), 1.0, col_hot)
        low = high
    pair_bf = pair[...].astype(jnp.float32).astype(jnp.bfloat16)
    hot_rows[...] = dot(row_hot.astype(jnp.bfloat16), pair_bf, NN).astype(jnp.bfloat16)
    hot_cols[...] = col_hot.astype(jnp.bfloat16)
    acc[...] = jnp.zeros_like(acc)
    part[...] = jnp.zeros_like(part)

    if Z > 2:
        relay(1)

    for cp in x_copies:
        cp.wait()

    def total_t(j, c):
        total = own[:, cols(j)]
        for n in range(A // 2 - 1):
            total = total + got2[n, :, cols(j)].astype(jnp.float32)
        hi = total.astype(jnp.bfloat16)
        t_hi[mine_rows, cols(j)] = hi
        t_lo[mine_rows, cols(j)] = (total - hi.astype(jnp.float32)).astype(jnp.bfloat16)
        return c

    lax.fori_loop(0, Q // QB, total_t, 0)
    t_copies = [rcopy(ref.at[mine_rows], ref.at[mine_rows], t_send.at[n], t_recv.at[n], {"aux": sibling})
                for n, ref in enumerate((t_hi, t_lo))]
    for cp in t_copies:
        cp.start()

    def back(half):
        def step(j, c):
            keys = pl.ds(pl.multiple_of(j * 256, 256), 256)
            fit[y, half, keys] = (dot(t_hi[half, :], metric[keys, :], NT)
                                  + dot(t_lo[half, :], metric[keys, :], NT)).astype(jnp.bfloat16)
            return c
        lax.fori_loop(0, PW // 256, step, 0)

    back(mine_rows)
    for cp in t_copies:
        cp.wait()
    back(other_rows)

    def u_copy(o):
        return rcopy(fit.at[y], fit.at[y], u_send.at[o - 1], u_recv.at[o - 1], {"ab": lax.rem(y + o, B)})

    for o in range(1, B):
        u_copy(o).start()
    for h in range(2, Z - 1):
        relay(h)
    own_copy.wait()
    for o in range(1, B):
        src = lax.rem(y - o + B, B)
        rcopy(fit.at[src], fit.at[src], u_send.at[o - 1], u_recv.at[o - 1], {"ab": lax.rem(y + o, B)}).wait_recv()
        u_copy(o).wait_send()

    NR = B * 2 * Z * GROUP
    NG = CB // GROUP
    NB = min(NR, 256)

    def ladder_chunk(k, carry):
        slot = lax.rem(k, 2)
        relay_chunk(Z - 1, k)
        lefts = gathered[:, chunk(k), :].reshape(Z * CB, PW)
        keep = dot(hot_rows[chunk(k), :], hot_cols[...], NN)
        for b in range(B):
            terms = dot(lefts, fit[b], NT).reshape(Z, CB, D) * keep[None]
            hi = terms.astype(jnp.bfloat16)
            lo = (terms - hi.astype(jnp.float32)).astype(jnp.bfloat16)
            for g in range(NG):
                ladder[g, b, 0] = hi[:, g * GROUP:(g + 1) * GROUP, :]
                ladder[g, b, 1] = lo[:, g * GROUP:(g + 1) * GROUP, :]
        amp_copy(k, slot).wait()

        def contract(g, c):
            kept = amps[slot, :, pl.ds(pl.multiple_of(g * GROUP, GROUP), GROUP), :].reshape(I * GROUP, D)
            flat = ladder[g].reshape(NR, D)
            for n in range(0, NR, NB):
                acc[:, n:n + NB] += dot(kept, flat[n:n + NB], NT)
            return c

        lax.fori_loop(0, NG, contract, 0)

        @pl.when(k + 2 < NC)
        def _():
            amp_copy(k + 2, slot).start()
        return carry

    lax.fori_loop(0, NC, ladder_chunk, 0)

    total = acc[...]
    same = (lax.rem(lax.broadcasted_iota(jnp.int32, total.shape, 0), GROUP)
            == lax.rem(lax.broadcasted_iota(jnp.int32, total.shape, 1), GROUP))
    total = jnp.sum(jnp.where(same, total, 0.0).reshape(I, GROUP, NR), axis=1)
    pick_row = lax.broadcasted_iota(jnp.int32, (Z * 8, NR), 0)
    pick_col = lax.broadcasted_iota(jnp.int32, (Z * 8, NR), 1)
    want = lax.rem(lax.div(pick_col, GROUP), Z) * 8 + lax.div(pick_col, 2 * Z * GROUP)
    pick = jnp.where(pick_row == want, 1.0, 0.0)
    sums = lax.dot_general(pick, total, NT, precision=lax.Precision.HIGHEST,
                           preferred_element_type=jnp.float32)
    part[:, :, :I] = sums.reshape(Z, 8, I)

    def fz(o):
        dest = lax.rem(z + o, Z)
        return rcopy(part.at[dest], got_z.at[o - 1], fz_send.at[o - 1], fz_recv.at[o - 1], {"cd": dest})

    for o in range(1, Z):
        fz(o).start()
    summed = part[z]
    for o in range(1, Z):
        fz(o).wait()
        summed = summed + got_z[o - 1]
    mine[...] = summed

    def fa(o):
        return rcopy(mine, got_ab.at[o - 1], fa_send.at[o - 1], fa_recv.at[o - 1], plane_peer(o))

    for o in range(1, A * B):
        fa(o).start()
    for o in range(1, A * B):
        fa(o).wait()
        summed = summed + got_ab[o - 1]
    row = lax.broadcasted_iota(jnp.int32, summed.shape, 0)
    out[...] = jnp.sum(jnp.where(row == y, summed, 0.0), axis=0, keepdims=True)[:, :I]

    for h in range(0, Z - 1):
        for way in (0, 1):
            o = z - h if way == 0 else z + h
            ok = (z - h >= 0) & (z < Z - 1) if way == 0 else (z + h < Z) & (z > 0)

            def drain(k, c, o=o, way=way, ok=ok):
                @pl.when(ok)
                def _():
                    push(gathered.at[o, chunk(k)], o, k, way).wait_send()
                return c
            lax.fori_loop(0, NC, drain, 0)


def body(left, right, metric, amplitudes, sizes, pair):
    A, Z, B = lax.axis_size("aux"), lax.axis_size("cd"), lax.axis_size("ab")
    a_local, C, PW = left.shape
    b_local, D, _ = right.shape
    Q = metric.shape[1]
    I = amplitudes.shape[0]
    T = pair.shape[0]
    CB = min(128, C)
    NC = C // CB
    H = D // 2
    NR = B * 2 * Z * GROUP
    X = max(A // 2 - 1, 1)
    bf, f32 = jnp.bfloat16, jnp.float32
    dma = pltpu.SemaphoreType.DMA
    vmem = pl.BlockSpec(memory_space=pltpu.VMEM)
    out = pl.pallas_call(
        functools.partial(kernel, A, Z, B, CB),
        out_shape=jax.ShapeDtypeStruct((1, I), f32),
        in_specs=[pl.BlockSpec(memory_space=pltpu.SMEM), vmem, vmem, vmem, vmem,
                  pl.BlockSpec(memory_space=pl.ANY)],
        out_specs=vmem,
        scratch_shapes=[
            pltpu.VMEM((Z, C, PW), bf),
            pltpu.VMEM((H, Q), bf), pltpu.VMEM((H, Q), bf), pltpu.VMEM((H, Q), f32),
            pltpu.VMEM((H, Q), bf), pltpu.VMEM((X, H, Q), bf),
            pltpu.VMEM((D, Q), bf), pltpu.VMEM((D, Q), bf),
            pltpu.VMEM((B, D, PW), bf),
            pltpu.VMEM((2, I, CB, D), bf),
            pltpu.VMEM((CB // GROUP, B, 2, Z, GROUP, D), bf),
            pltpu.VMEM((I * GROUP, NR), f32),
            pltpu.VMEM((C, T), bf), pltpu.VMEM((T, D), bf),
            pltpu.VMEM((Z, 8, 128), f32), pltpu.VMEM((max(Z - 1, 1), 8, 128), f32),
            pltpu.VMEM((8, 128), f32), pltpu.VMEM((max(A * B - 1, 1), 8, 128), f32),
            dma((2, Z, NC)), dma((Z, NC)), dma, dma, dma((X,)), dma((X,)), dma((2,)), dma((2,)),
            dma((max(B - 1, 1),)), dma((max(B - 1, 1),)), dma((2,)), dma,
            dma((max(Z - 1, 1),)), dma((max(Z - 1, 1),)),
            dma((max(A * B - 1, 1),)), dma((max(A * B - 1, 1),)),
        ],
        compiler_params=pltpu.CompilerParams(collective_id=0, has_side_effects=True,
                                             vmem_limit_bytes=60 * 1024 * 1024),
        name="ladder",
    )(sizes, left.reshape(C, PW), right.reshape(D, PW), metric, pair, amplitudes)
    return out.reshape(a_local, b_local, I)


def solution(mesh):
    return jax.shard_map(
        body,
        mesh=mesh,
        in_specs=(
            P("cd", "ab", "aux"),
            P("ab", "cd", "aux"),
            P("aux", None),
            P(None, "ab", "cd"),
            P(),
            P(),
        ),
        out_specs=P("cd", "ab", None),
        check_vma=False,
    )
```

time: 355 us -> 95.7 us (0.27)
  waiting for transfers between devices: 169 us -> 0 us
  Pallas kernels: 0 us -> 94.4 us
  matrix products: 82.5 us -> 0 us
  other arithmetic: 31.8 us -> 0 us
  local copies, waits for them, and re-layouts: 31.8 us -> 1.19 us
  blocking collectives: 25.1 us -> 0 us
  between operations: 13.2 us -> 0.01 us
    reduce_scatter x1 -> x0, waiting for transfers between devices: 100 us -> none  [body(): lax.psum_scatter(lax.dot_general(metric_factor, stacked, (((0,), (1,)), (...]
    pallas_call x0 -> x1, Pallas kernels: none -> 94.4 us  [body(): pl.pallas_call(functools.partial(kernel, A, Z, B, CB), out_shape=jax.Shap...]
    dot_general x11 -> x0, matrix products: 82.5 us -> none  [the longest x4 57.7 us: one_virtual(): lax.dot_general(ladder, kept, (((0, 2), (1, 2)), ((), ())), preferred_ele...]
    all_gather x2 -> x0, waiting for transfers between devices: 69.1 us -> none  [the longest x1 69.1 us: body(): lax.all_gather(left_fit, 'cd', axis=1, tiled=True)]
    mul x1 -> x0, other arithmetic: 29.4 us -> none  [body(): kept = amplitudes * keep_mask.astype(jnp.bfloat16)[None]]
    reshape x5 -> x0, local copies, waits for them, and re-layouts: 19.8 us -> none  [the longest x4 19.3 us: one_virtual(): ladder = ladder.astype(jnp.bfloat16).reshape(-1, b_count, d_width)]
    unnamed x1 -> x0, blocking collectives: 19 us -> none
    all_gather x1 -> x0, local copies, waits for them, and re-layouts: 6.35 us -> none  [body(): lax.all_gather(left_fit, 'cd', axis=1, tiled=True)]
  transfers between devices with their start and end apart: 3 -> 0, of which waited for: 2 -> 0; matrix products, arithmetic and copies ran while one was open for 10% -> 0% of each run, Pallas kernels for 0% -> 0%
where the time goes in v1:
time: 95.7 us; the launch traced here: 95.6 us
  Pallas kernels  94.4 us (99%)
  local copies, waits for them, and re-layouts  1.19 us (1%)
    pallas_call x1, Pallas kernels, body(): pl.pallas_call(functools.partial(kernel, A, Z, B, CB), out_shape=jax.Shap...  94.4 us

profile of v1, /device:TPU:0, one launch (start us, length us, event | category | flops | bytes accessed | tf_op | source)
XLA Modules:
  0.0 95.6 jit_solution(5433314651628485652)
XLA Ops:
  0.0 94.4 %ladder.1 = f32[1,32]{1,0:T(1,128)} custom-call(s32[16]{0:T(128)} %sizes.1, bf16[1024,512]{1,0:T(8,128)(2,1)} %bitcast.3, bf16[512,512]{1,0:T(8,128)(2,1)} %bitcast.4, bf16[512,2048]{1,0:T(8,128)(2,1)} %metric.1, s32[16,16]{1,0:T(8,128)} %pair.1, bf16[32,1024,512]{2,1,0:T(8,128)(2,1)} %amp.1), custom_call_target="tpu_custom_call" | custom-call | tf_op jit(solution)/shard_map/ladder/pallas_call | solution.py:300
  94.4 1.2 %copy.8 = f32[1,1,32]{2,1,0:T(1,128)} copy(f32[1,1,32]{2,1,0:T(1,128)} %bitcast.5) | data formatting | bytes 256

commit v2 on v1

--- a/solution.py
+++ b/solution.py
@@ -17,9 +17,9 @@
     return lax.dot_general(x, y, dims, preferred_element_type=jnp.float32)
 
 
-def kernel(A, Z, B, CB, sizes, left, right, metric, pair, amp, out,
-           gathered, send1, got1, own, chip, got2, t_hi, t_lo, fit, amps, ladder, acc,
-           hot_rows, hot_cols, part, got_z, mine, got_ab,
+def kernel(A, Z, B, CB, NX, sizes, left, right, metric, pair, amp, out,
+           gathered, send1, got1, own, chip, got2, right_fit, fit, amps, ladder, acc,
+           keep, part, got_z, mine, got_ab,
            z_send, z_recv, s_send, s_recv, x_send, x_recv, t_send, t_recv,
            u_send, u_recv, amp_sem, own_sem, fz_send, fz_recv, fa_send, fa_recv):
     aux, z, y = lax.axis_index("aux"), lax.axis_index("cd"), lax.axis_index("ab")
@@ -30,6 +30,7 @@
     T = pair.shape[0]
     NC = C // CB
     H = D // 2
+    HX = H // NX
     QB = min(512, Q)
     core = lax.rem(aux, 2)
     sibling = aux + 1 - 2 * core
@@ -96,12 +97,6 @@
                 def _():
                     push(gathered.at[o, chunk(k)], o, k, 1).start()
 
-    def relay(h):
-        def step(k, c):
-            relay_chunk(h, k)
-            return c
-        lax.fori_loop(0, NC, step, 0)
-
     mine_rows = pl.ds(pl.multiple_of(core * H, H), H)
     other_rows = pl.ds(pl.multiple_of((1 - core) * H, H), H)
 
@@ -113,27 +108,35 @@
         return c
 
     lax.fori_loop(0, Q // QB, fit_other, 0)
-    pair_copy = rcopy(send1, got1, s_send, s_recv, {"aux": sibling})
-    pair_copy.start()
+
+    def block(i):
+        return pl.ds(i * HX, HX)
+
+    pair_copies = [rcopy(send1.at[block(i)], got1.at[block(i)], s_send.at[i], s_recv.at[i], {"aux": sibling})
+                   for i in range(NX)]
+    for cp in pair_copies:
+        cp.start()
 
     def fit_own(j, c):
         own[:, cols(j)] = dot(right[mine_rows, :], metric[:, cols(j)], NN)
         return c
 
     lax.fori_loop(0, Q // QB, fit_own, 0)
-    pair_copy.wait()
-
-    def add_pair(j, c):
-        total = own[:, cols(j)] + got1[:, cols(j)].astype(jnp.float32)
-        own[:, cols(j)] = total
-        chip[:, cols(j)] = total.astype(jnp.bfloat16)
-        return c
-
-    lax.fori_loop(0, Q // QB, add_pair, 0)
-    x_copies = [rcopy(chip, got2.at[n], x_send.at[n], x_recv.at[n], {"aux": lax.rem(aux + 2 * n + 2, A)})
-                for n in range(A // 2 - 1)]
-    for cp in x_copies:
-        cp.start()
+    x_copies = []
+    for i in range(NX):
+        pair_copies[i].wait()
+
+        def add_pair(j, c, i=i):
+            total = own[block(i), cols(j)] + got1[block(i), cols(j)].astype(jnp.float32)
+            own[block(i), cols(j)] = total
+            chip[block(i), cols(j)] = total.astype(jnp.bfloat16)
+            return c
+
+        lax.fori_loop(0, Q // QB, add_pair, 0)
+        x_copies.append([rcopy(chip.at[block(i)], got2.at[n, block(i)], x_send.at[n, i], x_recv.at[n, i],
+                               {"aux": lax.rem(aux + 2 * n + 2, A)}) for n in range(A // 2 - 1)])
+        for cp in x_copies[i]:
+            cp.start()
 
     rows_at = y * C + lax.broadcasted_iota(jnp.int32, (C, T), 0)
     rows_tile = lax.broadcasted_iota(jnp.int32, (C, T), 1)
@@ -148,57 +151,103 @@
         col_hot = jnp.where((cols_tile == t) & (cols_at >= low) & (cols_at < high), 1.0, col_hot)
         low = high
     pair_bf = pair[...].astype(jnp.float32).astype(jnp.bfloat16)
-    hot_rows[...] = dot(row_hot.astype(jnp.bfloat16), pair_bf, NN).astype(jnp.bfloat16)
-    hot_cols[...] = col_hot.astype(jnp.bfloat16)
+    hot_rows = dot(row_hot.astype(jnp.bfloat16), pair_bf, NN).astype(jnp.bfloat16)
+    keep[...] = dot(hot_rows, col_hot.astype(jnp.bfloat16), NN)
     acc[...] = jnp.zeros_like(acc)
     part[...] = jnp.zeros_like(part)
 
-    if Z > 2:
-        relay(1)
-
-    for cp in x_copies:
-        cp.wait()
-
-    def total_t(j, c):
-        total = own[:, cols(j)]
-        for n in range(A // 2 - 1):
-            total = total + got2[n, :, cols(j)].astype(jnp.float32)
-        hi = total.astype(jnp.bfloat16)
-        t_hi[mine_rows, cols(j)] = hi
-        t_lo[mine_rows, cols(j)] = (total - hi.astype(jnp.float32)).astype(jnp.bfloat16)
-        return c
-
-    lax.fori_loop(0, Q // QB, total_t, 0)
-    t_copies = [rcopy(ref.at[mine_rows], ref.at[mine_rows], t_send.at[n], t_recv.at[n], {"aux": sibling})
-                for n, ref in enumerate((t_hi, t_lo))]
-    for cp in t_copies:
-        cp.start()
-
-    def back(half):
+    def t_copy(i):
+        return rcopy(right_fit.at[i, core], right_fit.at[i, core], t_send.at[i], t_recv.at[i], {"aux": sibling})
+
+    def u_rows(i, half):
+        return pl.ds(pl.multiple_of(half * H + i * HX, HX), HX)
+
+    def u_copy(i, half, o, owner):
+        place = fit.at[owner, u_rows(i, half)]
+        return rcopy(place, place, u_send.at[i, half, o - 1], u_recv.at[i, half, o - 1], {"ab": lax.rem(y + o, B)})
+
+    def finish_fit(i):
+        t_copy(i).wait()
+
         def step(j, c):
             keys = pl.ds(pl.multiple_of(j * 256, 256), 256)
-            fit[y, half, keys] = (dot(t_hi[half, :], metric[keys, :], NT)
-                                  + dot(t_lo[half, :], metric[keys, :], NT)).astype(jnp.bfloat16)
-            return c
+            both = dot(right_fit[i].reshape(4 * HX, Q), metric[keys, :], NT).reshape(2, 2, HX, 256)
+            both = (both[:, 0] + both[:, 1]).astype(jnp.bfloat16)
+            for half in range(2):
+                fit[y, u_rows(i, half), keys] = both[half]
+            return c
+
         lax.fori_loop(0, PW // 256, step, 0)
-
-    back(mine_rows)
-    for cp in t_copies:
-        cp.wait()
-    back(other_rows)
-
-    def u_copy(o):
-        return rcopy(fit.at[y], fit.at[y], u_send.at[o - 1], u_recv.at[o - 1], {"ab": lax.rem(y + o, B)})
-
-    for o in range(1, B):
-        u_copy(o).start()
+        for o in range(1, B):
+            for half in range(2):
+                u_copy(i, half, o, y).start()
+
+    for i in range(NX):
+        if Z > 2:
+            for k in range(i * NC // NX, (i + 1) * NC // NX):
+                relay_chunk(1, k)
+        for cp in x_copies[i]:
+            cp.wait()
+
+        def total_t(j, c, i=i):
+            total = own[block(i), cols(j)]
+            for n in range(A // 2 - 1):
+                total = total + got2[n, block(i), cols(j)].astype(jnp.float32)
+            hi = total.astype(jnp.bfloat16)
+            right_fit[i, core, 0, :, cols(j)] = hi
+            right_fit[i, core, 1, :, cols(j)] = (total - hi.astype(jnp.float32)).astype(jnp.bfloat16)
+            return c
+
+        lax.fori_loop(0, Q // QB, total_t, 0)
+        t_copy(i).start()
+        if i > 0:
+            finish_fit(i - 1)
+    finish_fit(NX - 1)
+    own_copy.wait()
+    for i in range(NX):
+        for o in range(1, B):
+            for half in range(2):
+                u_copy(i, half, o, y).wait_send()
+                u_copy(i, half, o, lax.rem(y - o + B, B)).wait_recv()
+
+    WIDE = min(2, NC)
+
+    def ladder_rows(o, k, chunks):
+        rows = pl.ds(pl.multiple_of(k * CB, CB), chunks * CB)
+        groups = pl.ds(k * (CB // GROUP), chunks * CB // GROUP)
+
+        @pl.when((o >= 0) & (o < Z))
+        def _():
+            kept = keep[rows, :]
+            for b in range(B):
+                terms = dot(gathered[o, rows, :], fit[b], NT) * kept
+                hi = terms.astype(jnp.bfloat16)
+                lo = (terms - hi.astype(jnp.float32)).astype(jnp.bfloat16)
+                ladder[groups, b, 0, o] = hi.reshape(-1, GROUP, D)
+                ladder[groups, b, 1, o] = lo.reshape(-1, GROUP, D)
+
+    def relay_wide(h, k):
+        for n in range(WIDE):
+            relay_chunk(h, k * WIDE + n)
+
+    def near(k, c):
+        ladder_rows(z, k * WIDE, WIDE)
+        if Z > 2:
+            ladder_rows(z - 1, k * WIDE, WIDE)
+            ladder_rows(z + 1, k * WIDE, WIDE)
+        if Z > 3:
+            relay_wide(2, k)
+        return c
+
+    lax.fori_loop(0, NC // WIDE, near, 0)
     for h in range(2, Z - 1):
-        relay(h)
-    own_copy.wait()
-    for o in range(1, B):
-        src = lax.rem(y - o + B, B)
-        rcopy(fit.at[src], fit.at[src], u_send.at[o - 1], u_recv.at[o - 1], {"ab": lax.rem(y + o, B)}).wait_recv()
-        u_copy(o).wait_send()
+        def far(k, c, h=h):
+            if h > 2:
+                relay_wide(h, k)
+            ladder_rows(z - h, k * WIDE, WIDE)
+            ladder_rows(z + h, k * WIDE, WIDE)
+            return c
+        lax.fori_loop(0, NC // WIDE, far, 0)
 
     NR = B * 2 * Z * GROUP
     NG = CB // GROUP
@@ -207,20 +256,14 @@
     def ladder_chunk(k, carry):
         slot = lax.rem(k, 2)
         relay_chunk(Z - 1, k)
-        lefts = gathered[:, chunk(k), :].reshape(Z * CB, PW)
-        keep = dot(hot_rows[chunk(k), :], hot_cols[...], NN)
-        for b in range(B):
-            terms = dot(lefts, fit[b], NT).reshape(Z, CB, D) * keep[None]
-            hi = terms.astype(jnp.bfloat16)
-            lo = (terms - hi.astype(jnp.float32)).astype(jnp.bfloat16)
-            for g in range(NG):
-                ladder[g, b, 0] = hi[:, g * GROUP:(g + 1) * GROUP, :]
-                ladder[g, b, 1] = lo[:, g * GROUP:(g + 1) * GROUP, :]
+        if Z > 1:
+            ladder_rows(z - (Z - 1), k, 1)
+            ladder_rows(z + (Z - 1), k, 1)
         amp_copy(k, slot).wait()
 
         def contract(g, c):
             kept = amps[slot, :, pl.ds(pl.multiple_of(g * GROUP, GROUP), GROUP), :].reshape(I * GROUP, D)
-            flat = ladder[g].reshape(NR, D)
+            flat = ladder[k * NG + g].reshape(NR, D)
             for n in range(0, NR, NB):
                 acc[:, n:n + NB] += dot(kept, flat[n:n + NB], NT)
             return c
@@ -292,13 +335,14 @@
     CB = min(128, C)
     NC = C // CB
     H = D // 2
+    NX = min(4, NC)
     NR = B * 2 * Z * GROUP
     X = max(A // 2 - 1, 1)
     bf, f32 = jnp.bfloat16, jnp.float32
     dma = pltpu.SemaphoreType.DMA
     vmem = pl.BlockSpec(memory_space=pltpu.VMEM)
     out = pl.pallas_call(
-        functools.partial(kernel, A, Z, B, CB),
+        functools.partial(kernel, A, Z, B, CB, NX),
         out_shape=jax.ShapeDtypeStruct((1, I), f32),
         in_specs=[pl.BlockSpec(memory_space=pltpu.SMEM), vmem, vmem, vmem, vmem,
                   pl.BlockSpec(memory_space=pl.ANY)],
@@ -307,16 +351,16 @@
             pltpu.VMEM((Z, C, PW), bf),
             pltpu.VMEM((H, Q), bf), pltpu.VMEM((H, Q), bf), pltpu.VMEM((H, Q), f32),
             pltpu.VMEM((H, Q), bf), pltpu.VMEM((X, H, Q), bf),
-            pltpu.VMEM((D, Q), bf), pltpu.VMEM((D, Q), bf),
+            pltpu.VMEM((NX, 2, 2, H // NX, Q), bf),
             pltpu.VMEM((B, D, PW), bf),
             pltpu.VMEM((2, I, CB, D), bf),
-            pltpu.VMEM((CB // GROUP, B, 2, Z, GROUP, D), bf),
+            pltpu.VMEM((C // GROUP, B, 2, Z, GROUP, D), bf),
             pltpu.VMEM((I * GROUP, NR), f32),
-            pltpu.VMEM((C, T), bf), pltpu.VMEM((T, D), bf),
+            pltpu.VMEM((C, D), f32),
             pltpu.VMEM((Z, 8, 128), f32), pltpu.VMEM((max(Z - 1, 1), 8, 128), f32),
             pltpu.VMEM((8, 128), f32), pltpu.VMEM((max(A * B - 1, 1), 8, 128), f32),
-            dma((2, Z, NC)), dma((Z, NC)), dma, dma, dma((X,)), dma((X,)), dma((2,)), dma((2,)),
-            dma((max(B - 1, 1),)), dma((max(B - 1, 1),)), dma((2,)), dma,
+            dma((2, Z, NC)), dma((Z, NC)), dma((NX,)), dma((NX,)), dma((X, NX)), dma((X, NX)), dma((NX,)), dma((NX,)),
+            dma((NX, 2, max(B - 1, 1))), dma((NX, 2, max(B - 1, 1))), dma((2,)), dma,
             dma((max(Z - 1, 1),)), dma((max(Z - 1, 1),)),
             dma((max(A * B - 1, 1),)), dma((max(A * B - 1, 1),)),
         ],

time: 95.7 us -> 93.6 us (0.978)
  Pallas kernels: 94.4 us -> 92.2 us
    pallas_call x1, Pallas kernels: 94.4 us -> 92.2 us  [body(): pl.pallas_call(functools.partial(kernel, A, Z, B, CB, NX), out_shape=jax....]
where the time goes in v2:
time: 93.6 us; the launch traced here: 93.4 us
  Pallas kernels  92.2 us (99%)
  local copies, waits for them, and re-layouts  1.19 us (1%)
    pallas_call x1, Pallas kernels, body(): pl.pallas_call(functools.partial(kernel, A, Z, B, CB, NX), out_shape=jax....  92.2 us

profile of v2, /device:TPU:0, one launch (start us, length us, event | category | flops | bytes accessed | tf_op | source)
XLA Modules:
  0.0 93.4 jit_solution(459333519814324420)
XLA Ops:
  0.0 92.2 %ladder.1 = f32[1,32]{1,0:T(1,128)} custom-call(s32[16]{0:T(128)} %sizes.1, bf16[1024,512]{1,0:T(8,128)(2,1)} %bitcast.3, bf16[512,512]{1,0:T(8,128)(2,1)} %bitcast.4, bf16[512,2048]{1,0:T(8,128)(2,1)} %metric.1, s32[16,16]{1,0:T(8,128)} %pair.1, bf16[32,1024,512]{2,1,0:T(8,128)(2,1)} %amp.1), custom_call_target="tpu_custom_call" | custom-call | tf_op jit(solution)/shard_map/ladder/pallas_call | solution.py:344
  92.3 1.2 %copy.8 = f32[1,1,32]{2,1,0:T(1,128)} copy(f32[1,1,32]{2,1,0:T(1,128)} %bitcast.5) | data formatting | bytes 256

commit v3 on v2

--- a/solution.py
+++ b/solution.py
@@ -231,12 +231,12 @@
             relay_chunk(h, k * WIDE + n)
 
     def near(k, c):
+        if Z > 3:
+            relay_wide(2, k)
         ladder_rows(z, k * WIDE, WIDE)
         if Z > 2:
             ladder_rows(z - 1, k * WIDE, WIDE)
             ladder_rows(z + 1, k * WIDE, WIDE)
-        if Z > 3:
-            relay_wide(2, k)
         return c
 
     lax.fori_loop(0, NC // WIDE, near, 0)

time: 93.6 us -> 93.8 us (level)
  no operation moved by 1% of the time
where the time goes in v3:
time: 93.8 us; the launch traced here: 93.6 us
  Pallas kernels  92.4 us (99%)
  local copies, waits for them, and re-layouts  1.19 us (1%)
    pallas_call x1, Pallas kernels, body(): pl.pallas_call(functools.partial(kernel, A, Z, B, CB, NX), out_shape=jax....  92.4 us

profile of v3, /device:TPU:0, one launch (start us, length us, event | category | flops | bytes accessed | tf_op | source)
XLA Modules:
  0.0 93.6 jit_solution(2430001565033090189)
XLA Ops:
  0.0 92.4 %ladder.1 = f32[1,32]{1,0:T(1,128)} custom-call(s32[16]{0:T(128)} %sizes.1, bf16[1024,512]{1,0:T(8,128)(2,1)} %bitcast.3, bf16[512,512]{1,0:T(8,128)(2,1)} %bitcast.4, bf16[512,2048]{1,0:T(8,128)(2,1)} %metric.1, s32[16,16]{1,0:T(8,128)} %pair.1, bf16[32,1024,512]{2,1,0:T(8,128)(2,1)} %amp.1), custom_call_target="tpu_custom_call" | custom-call | tf_op jit(solution)/shard_map/ladder/pallas_call | solution.py:344
  92.4 1.2 %copy.8 = f32[1,1,32]{2,1,0:T(1,128)} copy(f32[1,1,32]{2,1,0:T(1,128)} %bitcast.5) | data formatting | bytes 256
